TPU v7x, 32 devices: a whole 2x2x4 slice. The times are simulated.
32 devices in a mesh: bins: 4 (over y, x), batch: 4 (over z), fsdp: 2 (over core).
Axes of the slice: x: 2, y: 2, z: 4, core: 2. Of those that a mesh axis runs over, the one named last changes fastest.
Arguments:
- track_in: bfloat16 [64, 1024, 768], P(('batch', 'fsdp'), 'bins'), may hold values from -6 to 6
- black_mask: int32 [64, 1024], P(('batch', 'fsdp'), 'bins'), may hold values 0 or 1
- unmap_mask: int32 [64, 1024], P(('batch', 'fsdp'), 'bins'), may hold values 0 or 1
- seq_valid: int32 [64], P(('batch', 'fsdp')), may hold values from 256 to 1024
- dilated_weight: float32 [2304, 384], P(('batch', 'fsdp')), may hold values from -0.125 to 0.125
- point_weight: float32 [384, 768], P(('batch', 'fsdp')), may hold values from -0.30618622 to 0.30618622
- point_bias: float32 [768], P(('batch', 'fsdp')), may hold values from -3 to 3
- gain_first: float32 [768], P(('batch', 'fsdp')), may hold values from 0.5 to 2
- shift_first: float32 [768], P(('batch', 'fsdp')), may hold values from -3 to 3
- gain_second: float32 [384], P(('batch', 'fsdp')), may hold values from 0.5 to 2
- shift_second: float32 [384], P(('batch', 'fsdp')), may hold values from -3 to 3
- out_grad: bfloat16 [64, 1024, 768], P(('batch', 'fsdp'), 'bins'), may hold values from -8 to 8
Outputs:
- block_out: bfloat16 [64, 1024, 768], P(('batch', 'fsdp'), 'bins')
- input_grad: bfloat16 [64, 1024, 768], P(('batch', 'fsdp'), 'bins')
- dilated_grad: float32 [2304, 384], P(('batch', 'fsdp'))
- point_grad: float32 [384, 768], P(('batch', 'fsdp'))
- bias_grad: float32 [768], P(('batch', 'fsdp'))
- gain_first_grad: float32 [768], P(('batch', 'fsdp'))
- shift_first_grad: float32 [768], P(('batch', 'fsdp'))
- gain_second_grad: float32 [384], P(('batch', 'fsdp'))
- shift_second_grad: float32 [384], P(('batch', 'fsdp'))
All inputs are finite; a program needn't handle non-finite values. No bound on the sum of `black_mask` or of `unmap_mask` on one device may be relied on, other than what follows from the above.
Results may differ from a plain program's by a relative error of at most 0.0074.
Values may be sent and summed in bfloat16 or wider, within the bound.
A program may use at most 128 MiB of HBM per device.

v0:
```python
import jax
import jax.numpy as jnp
from jax import lax
from jax.sharding import PartitionSpec as P

DILATION_STEP = 26
norm_eps = 1e-05


def extended(block, sides, width):
    for axis, dim in sides:
        count = lax.axis_size(axis)
        forward = [(i, i + 1) for i in range(count - 1)]
        backward = [(target, source) for source, target in forward]
        low = lax.ppermute(
            lax.slice_in_dim(block, block.shape[dim] - width, None, axis=dim), axis, forward
        )
        high = lax.ppermute(lax.slice_in_dim(block, 0, width, axis=dim), axis, backward)
        block = jnp.concatenate([low, block, high], axis=dim)
    return block


def activate(values):
    return values * jax.nn.sigmoid(1.702 * values)


def slope(values):
    sigma = jax.nn.sigmoid(1.702 * values)
    return sigma + 1.702 * values * sigma * (1.0 - sigma)


def moments(values, valid, local_count):
    total, count = lax.psum(
        (jnp.sum(values * valid, axis=0), local_count), ("bins", "batch", "fsdp")
    )
    mean = total / count
    centred = values - mean
    spread = lax.psum(jnp.sum(centred * centred * valid, axis=0), ("bins", "batch", "fsdp"))
    variance = spread / count
    scale = lax.rsqrt(variance + norm_eps)
    return (centred * scale, scale, count)


def norm_back(grad_out, normed, scale, gain, valid, count):
    total, cross = lax.psum(
        (jnp.sum(grad_out, axis=0), jnp.sum(grad_out * normed, axis=0)), ("bins", "batch", "fsdp")
    )
    grad_in = scale * gain * (grad_out - valid * (total + normed * cross) / count)
    return (grad_in, total, cross)


def contract_rows(left, right):
    return lax.dot_general(
        left, right, (((0,), (0,)), ((), ())), preferred_element_type=jnp.float32
    )


def local(
    track_in,
    black_mask,
    unmap_mask,
    seq_valid,
    dilated_weight,
    point_weight,
    point_bias,
    gain_first,
    shift_first,
    gain_second,
    shift_second,
    out_grad,
):
    sequence_count, count_of_bins, channel_count = track_in.shape
    row_count = sequence_count * count_of_bins
    bf = jnp.bfloat16
    gathered_taps = (
        lax.all_gather(dilated_weight.astype(bf), ("batch", "fsdp"), axis=0, tiled=True),
        lax.all_gather(point_weight.astype(bf), ("batch", "fsdp"), axis=0, tiled=True),
        lax.all_gather(point_bias.astype(bf), ("batch", "fsdp"), axis=0, tiled=True),
        lax.all_gather(gain_first.astype(bf), ("batch", "fsdp"), axis=0, tiled=True),
        lax.all_gather(shift_first.astype(bf), ("batch", "fsdp"), axis=0, tiled=True),
        lax.all_gather(gain_second.astype(bf), ("batch", "fsdp"), axis=0, tiled=True),
        lax.all_gather(shift_second.astype(bf), ("batch", "fsdp"), axis=0, tiled=True),
    )
    dilation_weight = gathered_taps[0]
    pointwise_weight = gathered_taps[1]
    hidden_state = pointwise_weight.shape[0]
    bias_vector = gathered_taps[2].astype(jnp.float32)
    first_gain = gathered_taps[3].astype(jnp.float32)
    first_offset = gathered_taps[4].astype(jnp.float32)
    second_gain = gathered_taps[5].astype(jnp.float32)
    second_offset = gathered_taps[6].astype(jnp.float32)
    place = lax.axis_index("bins") * count_of_bins + lax.broadcasted_iota(
        jnp.int32, (sequence_count, count_of_bins), 1
    )
    keep = (black_mask == 0) & (unmap_mask == 0) & (place < seq_valid[:, None])
    valid = keep.astype(jnp.float32).reshape(row_count, 1)
    local_count = jnp.sum(valid)
    input_signal = track_in.reshape(row_count, channel_count).astype(jnp.float32)
    normed_one, scale_one, count = moments(input_signal, valid, local_count)
    pre_one = normed_one * first_gain + first_offset
    first_hidden = activate(pre_one).astype(bf)
    first_padded = extended(
        first_hidden.reshape(sequence_count, count_of_bins, channel_count),
        (("bins", 1),),
        DILATION_STEP,
    )
    kernel_taps = jnp.concatenate(
        [
            first_padded[
                :,
                kernel_tap_index * DILATION_STEP : kernel_tap_index * DILATION_STEP + count_of_bins,
                :,
            ]
            for kernel_tap_index in range(3)
        ],
        axis=2,
    ).reshape(row_count, 3 * channel_count)
    convolution_output = jnp.dot(kernel_taps, dilation_weight, preferred_element_type=jnp.float32)
    normed_two, scale_two, count_again = moments(convolution_output, valid, local_count)
    pre_two = normed_two * second_gain + second_offset
    hidden_two = activate(pre_two).astype(bf)
    branch = jnp.dot(hidden_two, pointwise_weight, preferred_element_type=jnp.float32)
    block_out = (
        (input_signal + branch + bias_vector)
        .astype(bf)
        .reshape(sequence_count, count_of_bins, channel_count)
    )
    grad = out_grad.reshape(row_count, channel_count) * keep.reshape(row_count, 1).astype(bf)
    point_local = contract_rows(hidden_two, grad)
    bias_local = jnp.sum(grad, axis=0, dtype=jnp.float32)
    grad_two = jnp.dot(grad, pointwise_weight.T, preferred_element_type=jnp.float32) * slope(
        pre_two
    )
    convolution_gradient, shift_two_total, gain_two_total = norm_back(
        grad_two, normed_two, scale_two, second_gain, valid, count
    )
    convolution_gradient = convolution_gradient.astype(bf)
    dilated_local = contract_rows(kernel_taps, convolution_gradient)
    padded_gradient = extended(
        convolution_gradient.reshape(sequence_count, count_of_bins, hidden_state),
        (("bins", 1),),
        DILATION_STEP,
    )
    back_taps = jnp.concatenate(
        [
            padded_gradient[
                :,
                (2 - kernel_tap_index) * DILATION_STEP : (2 - kernel_tap_index) * DILATION_STEP
                + count_of_bins,
                :,
            ]
            for kernel_tap_index in range(3)
        ],
        axis=2,
    ).reshape(row_count, 3 * hidden_state)
    weight_backward = jnp.transpose(
        dilation_weight.reshape(3, channel_count, hidden_state), (0, 2, 1)
    ).reshape(3 * hidden_state, channel_count)
    grad_one = jnp.dot(back_taps, weight_backward, preferred_element_type=jnp.float32) * slope(
        pre_one
    )
    input_part, shift_one_total, gain_one_total = norm_back(
        grad_one, normed_one, scale_one, first_gain, valid, count
    )
    input_grad = (
        (grad.astype(jnp.float32) + input_part)
        .astype(bf)
        .reshape(sequence_count, count_of_bins, channel_count)
    )
    local_grads = (dilated_local, point_local, bias_local)
    summed = lax.psum((local_grads[0], local_grads[1], local_grads[2]), "bins")
    shares = (
        lax.psum_scatter(summed[0], ("batch", "fsdp"), scatter_dimension=0, tiled=True),
        lax.psum_scatter(summed[1], ("batch", "fsdp"), scatter_dimension=0, tiled=True),
        lax.psum_scatter(summed[2], ("batch", "fsdp"), scatter_dimension=0, tiled=True),
    )
    owner = lax.axis_index(("batch", "fsdp"))
    group_size = lax.axis_size(("batch", "fsdp"))
    wide_share = channel_count // group_size
    narrow_share = hidden_state // group_size
    gain_first_grad = lax.dynamic_slice_in_dim(gain_one_total, owner * wide_share, wide_share)
    shift_first_grad = lax.dynamic_slice_in_dim(shift_one_total, owner * wide_share, wide_share)
    gain_second_grad = lax.dynamic_slice_in_dim(gain_two_total, owner * narrow_share, narrow_share)
    shift_second_grad = lax.dynamic_slice_in_dim(
        shift_two_total, owner * narrow_share, narrow_share
    )
    return (
        block_out,
        input_grad,
        shares[0],
        shares[1],
        shares[2],
        gain_first_grad,
        shift_first_grad,
        gain_second_grad,
        shift_second_grad,
    )


def solution(mesh):
    return jax.shard_map(
        local,
        mesh=mesh,
        in_specs=(
            P(("batch", "fsdp"), "bins", None),
            P(("batch", "fsdp"), "bins"),
            P(("batch", "fsdp"), "bins"),
            P(("batch", "fsdp")),
            P(("batch", "fsdp"), None),
            P(("batch", "fsdp"), None),
            P(("batch", "fsdp")),
            P(("batch", "fsdp")),
            P(("batch", "fsdp")),
            P(("batch", "fsdp")),
            P(("batch", "fsdp")),
            P(("batch", "fsdp"), "bins", None),
        ),
        out_specs=(
            P(("batch", "fsdp"), "bins", None),
            P(("batch", "fsdp"), "bins", None),
            P(("batch", "fsdp"), None),
            P(("batch", "fsdp"), None),
            P(("batch", "fsdp")),
            P(("batch", "fsdp")),
            P(("batch", "fsdp")),
            P(("batch", "fsdp")),
            P(("batch", "fsdp")),
        ),
        check_vma=False,
    )
```

profile of v0, /device:TPU:0, one launch (start us, length us, event | category | flops | bytes accessed | tf_op | source)
XLA Modules:
  0.0 466.3 jit_solution(5711937940642805629)
XLA Ops:
  7.2 1.9 convert_element_type.96
  9.1 0.0 reduce-scatter.5.cloned.1.call-start
  9.2 0.8 fusion.46
  10.0 0.6 convert_reduce_fusion.1
  10.6 1.3 fusion.49
  13.2 0.7 convert_element_type.103
  13.9 0.7 convert_element_type.91
  14.6 0.7 convert_element_type.93
  15.2 0.7 convert_element_type.97
  15.9 0.7 convert_element_type.99
  16.5 0.2 dynamic-update-slice.3
  16.7 0.2 dynamic-update-slice.2
  16.9 0.2 dynamic-update-slice.1
  17.2 0.2 dynamic-update-slice.4
  17.4 0.2 dynamic-update-slice
  17.6 19.0 %all-reduce.10 = (bf16[768]{0:T(1024)(128)(2,1)S(1)}, bf16[768]{0:T(1024)(128)(2,1)S(1)}, bf16[768]{0:T(1024)(128)(2,1)S(1)}, bf16[384]{0:T(512)(128)(2,1)S(1)}, bf16[384]{0:T(512)(128)(2,1)S(1)}) all-reduce(bf16[768]{0:T(1024)(128)(2,1)S(1)} %dynamic-update-slice.4, ...), channel_id=1, replica_groups=mesh['bins'=4,'batch'=4,'fsdp'=2] {'batch','fsdp'}, use_global_device_ids=true, to_apply=%add.4 | all-reduce | flops 3072 | bytes 12288
  36.7 2.6 fusion.13
  39.3 38.0 %all-reduce.8 = (f32[768]{0:T(1024)S(1)}, f32[]{:T(128)}) all-reduce(f32[768]{0:T(1024)S(1)} %fusion.13, f32[]{:T(128)} %convert_reduce_fusion.1), channel_id=1, replica_groups=mesh['bins'=4,'batch'=4,'fsdp'=2] {'bins','batch','fsdp'}, use_global_device_ids=true, to_apply=%region_1.0 | all-reduce | flops 769 | bytes 6152 | tf_op jit(solution)/shard_map/psum | solution.py:33
  77.3 0.6 broadcast_divide_fusion
  77.9 1.1 fusion.3
  79.0 41.7 %psum.89 = f32[768]{0:T(1024)S(1)} all-reduce(f32[768]{0:T(1024)S(1)} %fusion.3), channel_id=1, replica_groups=mesh['bins'=4,'batch'=4,'fsdp'=2] {'bins','batch','fsdp'}, use_global_device_ids=true, to_apply=%region_5.0 | all-reduce | flops 768 | bytes 6144 | tf_op jit(solution)/shard_map/psum | solution.py:38
  120.6 1.2 convert_multiply_fusion.1
  121.9 2.4 fusion.12
  124.4 0.1 fusion.47
  124.5 4.2 collective-permute-start
  128.7 1.3 collective-permute-start.1
  130.0 2.3 bitcast_multiply_fusion
  132.3 15.8 %all_gather.26 = bf16[384,768]{1,0:T(8,128)(2,1)} all-gather(bf16[48,768]{1,0:T(8,128)(2,1)S(1)} %convert_element_type.102), channel_id=1, replica_groups=mesh['bins'=4,'batch'=4,'fsdp'=2] {'batch','fsdp'}, dimensions={0}, use_global_device_ids=true | all-gather | bytes 663552 | tf_op jit(solution)/shard_map/all_gather | solution.py:77
  148.2 3.6 pad_maximum_fusion.4
  151.8 9.3 %multiply_reduce_fusion.2 = (f32[384]{0:T(512)S(1)}, f32[2048,384]{1,0:T(8,128)}) fusion(f32[2048]{0:T(1024)S(1)} %bitcast.82, bf16[2304,384]{1,0:T(8,128)(2,1)} %all-gather.2.cloned.1.call-done, bf16[2048,768]{1,0:T(8,128)(2,1)} %bitcast.75, bf16[2048,768]{1,0:T(8,128)(2,1)} %bitcast.69, bf16[2048,768]{1,0:T(8,128)(2,1)} %bitcast.73), kind=kOutput, calls=%fused_computation.55 | convolution fusion | flops 3653762560 | bytes 14362112 | tf_op jit(solution)/shard_map/dot_general | solution.py:118
  161.0 39.7 %psum.90 = f32[384]{0:T(512)S(1)} all-reduce(f32[384]{0:T(512)S(1)} %get-tuple-element.45), channel_id=1, replica_groups=mesh['bins'=4,'batch'=4,'fsdp'=2] {'bins','batch','fsdp'}, use_global_device_ids=true, to_apply=%region_7.0 | all-reduce | flops 384 | bytes 3072 | tf_op jit(solution)/shard_map/psum | solution.py:33
  200.7 0.6 broadcast_divide_fusion.1
  201.4 2.3 multiply_reduce_fusion.1
  203.7 41.8 %psum.91 = f32[384]{0:T(512)S(1)} all-reduce(f32[384]{0:T(512)S(1)} %multiply_reduce_fusion.1), channel_id=1, replica_groups=mesh['bins'=4,'batch'=4,'fsdp'=2] {'bins','batch','fsdp'}, use_global_device_ids=true, to_apply=%region_9.0 | all-reduce | flops 384 | bytes 3072 | tf_op jit(solution)/shard_map/psum | solution.py:38
  245.6 0.7 convert_multiply_fusion.2
  246.2 5.5 %fusion.43 = f32[384,768]{1,0:T(8,128)} fusion(bf16[2048,768]{1,0:T(8,128)(2,1)} %bitcast_multiply_fusion, f32[2048,384]{1,0:T(8,128)} %get-tuple-element.46, f32[384]{0:T(512)S(1)} %convert_element_type.100, f32[384]{0:T(512)S(1)} %convert_element_type.98, f32[384]{0:T(512)S(1)} %get-tuple-element.31, f32[384]{0:T(512)S(1)} %broadcast_divide_fusion.1), kind=kOutput, calls=%fused_computation.73 | convolution fusion | flops 1215823872 | bytes 7477248 | tf_op jit(solution)/shard_map/dot_general | solution.py:53
  251.7 0.0 reduce-scatter.3.cloned.1.call-start
  251.8 7.8 %fusion.45 = (f32[384]{0:T(512)S(1)}, f32[384]{0:T(512)S(1)}, f32[2048,384]{1,0:T(8,128)}) fusion(f32[384]{0:T(512)S(1)} %get-tuple-element.31, f32[2048,384]{1,0:T(8,128)} %get-tuple-element.46, f32[384]{0:T(512)S(1)} %broadcast_divide_fusion.1, f32[384]{0:T(512)S(1)} %convert_element_type.100, f32[384]{0:T(512)S(1)} %convert_element_type.98, ...), kind=kOutput, calls=%fused_computation.75 | convolution fusion | flops 1220541696 | bytes 10036224 | tf_op jit(solution)/shard_map/dot_general | solution.py:131
  259.6 38.6 %all-reduce.7 = (f32[384]{0:T(512)S(1)}, f32[384]{0:T(512)S(1)}) all-reduce(f32[384]{0:T(512)S(1)} %get-tuple-element.12, f32[384]{0:T(512)S(1)} %get-tuple-element.11), channel_id=1, replica_groups=mesh['bins'=4,'batch'=4,'fsdp'=2] {'bins','batch','fsdp'}, use_global_device_ids=true, to_apply=%region_13.0 | all-reduce | flops 768 | bytes 6144 | tf_op jit(solution)/shard_map/psum | solution.py:45
  298.3 4.5 multiply_convert_fusion
  302.8 1.1 copy-done.4
  303.9 6.8 %fusion.36 = f32[2304,384]{1,0:T(8,128)} fusion(bf16[2048,384]{1,0:T(8,128)(2,1)S(1)} %multiply_convert_fusion, bf16[2048,768]{1,0:T(8,128)(2,1)} %bitcast.76, bf16[2048,768]{1,0:T(8,128)(2,1)S(1)} %bitcast.70, bf16[2048,768]{1,0:T(8,128)(2,1)S(1)} %bitcast.74), kind=kOutput, calls=%fused_computation.43 | convolution fusion | flops 3652190208 | bytes 14548992 | tf_op jit(solution)/shard_map/dot_general | solution.py:53
  310.7 0.0 all-reduce.13.cloned.1.call-start
  310.8 0.6 convert_element_type.104
  312.1 2.6 convert_reduce_fusion
  314.6 14.9 %all-reduce.5 = f32[768]{0:T(1024)S(1)} all-reduce(f32[768]{0:T(1024)S(1)} %convert_reduce_fusion), channel_id=4, replica_groups=mesh['bins'=4,'batch'=4,'fsdp'=2] {'batch','fsdp'}, use_global_device_ids=true, to_apply=%region_24.0.clone | all-reduce | flops 768 | bytes 6144
  329.5 0.1 dynamic-slice.6
  329.6 10.6 %psum.101 = f32[96]{0:T(128)} all-reduce(f32[96]{0:T(128)S(1)} %dynamic-slice.6), channel_id=1, replica_groups=mesh['bins'=4,'batch'=4,'fsdp'=2] {'bins'}, use_global_device_ids=true, to_apply=%region_23.0 | all-reduce | flops 96 | bytes 768 | tf_op jit(solution)/shard_map/psum | solution.py:171
  340.2 1.8 fusion.48
  342.0 1.3 collective-permute-start.2
  343.3 4.8 %collective-permute-start.3 = (bf16[8,26,384]{2,1,0:T(8,128)(2,1)}, bf16[8,26,384]{2,1,0:T(8,128)(2,1)S(1)}, u32[]{:S(2)}, u32[]{:S(2)}) collective-permute-start(bf16[8,26,384]{2,1,0:T(8,128)(2,1)} %get-tuple-element.39), channel_id=1, source_target_pairs={{0,8},{8,16},{16,24},{1,9},{9,17},{17,25},{2,10},{10,18},{18,26},{... | collective-permute-start | bytes 479240 | tf_op jit(solution)/shard_map/ppermute | solution.py:15
  348.1 6.4 %fusion.15 = bf16[2048,768]{1,0:T(8,128)(2,1)} fusion(bf16[8,256,768]{2,1,0:T(8,128)(2,1)S(1)} %copy-done, bf16[384,768]{1,0:T(8,128)(2,1)} %all_gather.26, f32[768]{0:T(1024)} %convert_element_type.104, f32[2048,384]{1,0:T(8,128)} %get-tuple-element.46, f32[384]{0:T(512)} %copy-done.20, f32[384]{0:T(512)} %copy-done.21, f32[384]{0:T(512)} %copy-done.17, ...), kind=kOutput, calls=%fused_computation.20 | convolution fusion | flops 1222115328 | bytes 10036224 | tf_op jit(solution)/shard_map/dot_general | solution.py:122
  354.5 1.2 dynamic_slice.15
  355.7 1.3 dynamic_slice.14
  356.9 3.8 copy.22
  360.8 3.1 pad_maximum_fusion.6
  364.0 8.4 %fusion.44 = (f32[768]{0:T(1024)S(1)}, f32[768]{0:T(1024)S(1)}, f32[2048,768]{1,0:T(8,128)}) fusion(f32[768]{0:T(1024)S(1)} %get-tuple-element.29, f32[768]{0:T(1024)S(1)} %broadcast_divide_fusion, bf16[8,256,768]{2,1,0:T(8,128)(2,1)S(1)} %copy-done, f32[768]{0:T(1024)S(1)} %copy-done.13, f32[768]{0:T(1024)S(1)} %copy-done.15, ...), kind=kOutput, calls=%fused_computation.74 | convolution fusion | flops 3664771584 | bytes 15943680 | tf_op jit(solution)/shard_map/dot_general | solution.py:159
  372.3 37.0 %all-reduce.6 = (f32[768]{0:T(1024)S(1)}, f32[768]{0:T(1024)S(1)}) all-reduce(f32[768]{0:T(1024)S(1)} %get-tuple-element.10, f32[768]{0:T(1024)S(1)} %get-tuple-element.9), channel_id=1, replica_groups=mesh['bins'=4,'batch'=4,'fsdp'=2] {'bins','batch','fsdp'}, use_global_device_ids=true, to_apply=%region_17.0 | all-reduce | flops 1536 | bytes 12288 | tf_op jit(solution)/shard_map/psum | solution.py:45
  409.4 6.9 %fusion.29 = bf16[2048,768]{1,0:T(8,128)(2,1)} fusion(f32[2048,768]{1,0:T(8,128)} %get-tuple-element.48, bf16[8,256,768]{2,1,0:T(8,128)(2,1)S(1)} %copy-done, f32[]{:T(128)} %get-tuple-element.18, f32[768]{0:T(1024)S(1)} %get-tuple-element.13, f32[768]{0:T(1024)S(1)} %get-tuple-element.14, f32[2048]{0:T(1024)S(1)} %bitcast.85, ...), kind=kLoop, calls=%fused_computation.36 | loop fusion | flops 20447232 | bytes 15756292 | tf_op jit(solution)/shard_map/convert_element_type | solution.py:167
  416.2 0.6 dynamic_slice.13
  416.8 0.6 dynamic_slice.12
  417.4 39.0 %all-reduce.13.cloned.1.call-done = (f32[288,384]{1,0:T(8,128)}, f32[48,768]{1,0:T(8,128)}) async-done(((f32[288,384]{1,0:T(8,128)}, f32[48,768]{1,0:T(8,128)}), (f32[288,384]{1,0:T(8,128)}, f32[48,768]{1,0:T(8,128)})) %all-reduce.13.cloned.1.call-update) | async-done | bytes 589840 | tf_op jit(solution)/shard_map/psum | solution.py:171
  456.4 1.8 copy.32
  458.2 1.6 copy.33
  (69 shorter events, 0.3 us)
Async XLA Ops:
  7.2 70.7 %copy-start = (bf16[8,256,768]{2,1,0:T(8,128)(2,1)S(1)}, bf16[8,256,768]{2,1,0:T(8,128)(2,1)}, u32[]{:S(2)}) copy-start(bf16[8,256,768]{2,1,0:T(8,128)(2,1)} %param.12) | copy-start | bytes 9437188
  7.2 144.6 %all-gather.2.cloned.1.call-start = ((), (), s32[]{:S(2)}) async-start(), calls=%async_computation.2 | async-start | bytes 1990656 | tf_op jit(solution)/shard_map/all_gather | solution.py:76
  9.1 400.2 %reduce-scatter.5.cloned.1.call-start = ((), (), s32[]{:S(2)}) async-start(), calls=%async_computation.4 | async-start | bytes 1327104 | tf_op jit(solution)/shard_map/reduce_scatter | solution.py:174
  36.6 85.3 %copy-start.12 = (f32[768]{0:T(1024)}, f32[768]{0:T(1024)S(1)}, u32[]{:S(2)}) copy-start(f32[768]{0:T(1024)S(1)} %convert_element_type.94) | copy-start | bytes 9220
  36.6 85.3 %copy-start.14 = (f32[768]{0:T(1024)}, f32[768]{0:T(1024)S(1)}, u32[]{:S(2)}) copy-start(f32[768]{0:T(1024)S(1)} %convert_element_type.92) | copy-start | bytes 9220
  121.9 8.1 %copy-start.1 = (bf16[8,256,768]{2,1,0:T(8,128)(2,1)S(1)}, bf16[8,256,768]{2,1,0:T(8,128)(2,1)}, u32[]{:S(2)}) copy-start(bf16[8,256,768]{2,1,0:T(8,128)(2,1)} %param.23) | copy-start | bytes 9437188
  124.3 23.8 %copy-start.2 = (bf16[8,256,768]{2,1,0:T(8,128)(2,1)}, bf16[8,256,768]{2,1,0:T(8,128)(2,1)S(1)}, u32[]{:S(2)}) copy-start(bf16[8,256,768]{2,1,0:T(8,128)(2,1)S(1)} %fusion.12) | copy-start | bytes 9437188
  124.5 23.7 %collective-permute-start = (bf16[8,26,768]{2,1,0:T(8,128)(2,1)S(1)}, bf16[8,26,768]{2,1,0:T(8,128)(2,1)S(1)}, u32[]{:S(2)}, u32[]{:S(2)}) collective-permute-start(bf16[8,26,768]{2,1,0:T(8,128)(2,1)S(1)} %get-tuple-element.34), channel_id=1, source_target_pairs={{0,8},{8,16},{16,24},{1,9},{9,17},{17,25},{2,10},{10,18},{18,26},{... | collective-permute-start | bytes 958472 | tf_op jit(solution)/shard_map/ppermute | solution.py:15
  128.7 19.5 %collective-permute-start.1 = (bf16[8,26,768]{2,1,0:T(8,128)(2,1)S(1)}, bf16[8,26,768]{2,1,0:T(8,128)(2,1)S(1)}, u32[]{:S(2)}, u32[]{:S(2)}) collective-permute-start(bf16[8,26,768]{2,1,0:T(8,128)(2,1)S(1)} %get-tuple-element.35), channel_id=1, source_target_pairs={{8,0},{16,8},{24,16},{9,1},{17,9},{25,17},{10,2},{18,10},{26,18},{... | collective-permute-start | bytes 958472 | tf_op jit(solution)/shard_map/ppermute | solution.py:18
  130.0 2.3 copy-start.9
  130.0 2.3 copy-start.8
  132.3 119.5 %copy-start.20 = (f32[384]{0:T(512)}, f32[384]{0:T(512)S(1)}, u32[]{:S(2)}) copy-start(f32[384]{0:T(512)S(1)} %convert_element_type.100) | copy-start | bytes 4612
  132.3 119.5 %copy-start.21 = (f32[384]{0:T(512)}, f32[384]{0:T(512)S(1)}, u32[]{:S(2)}) copy-start(f32[384]{0:T(512)S(1)} %convert_element_type.98) | copy-start | bytes 4612
  201.4 96.8 %copy-start.11 = (f32[384]{0:T(512)}, f32[384]{0:T(512)S(1)}, u32[]{:S(2)}) copy-start(f32[384]{0:T(512)S(1)} %broadcast_divide_fusion.1) | copy-start | bytes 4612
  246.2 52.0 %copy-start.17 = (f32[384]{0:T(512)}, f32[384]{0:T(512)S(1)}, u32[]{:S(2)}) copy-start(f32[384]{0:T(512)S(1)} %get-tuple-element.31) | copy-start | bytes 4612
  251.7 157.6 %reduce-scatter.3.cloned.1.call-start = ((), (), s32[]{:S(2)}) async-start(), calls=%async_computation.3 | async-start | bytes 3981312 | tf_op jit(solution)/shard_map/reduce_scatter | solution.py:173
  298.2 4.6 copy-start.18
  298.2 4.6 copy-start.19
  298.2 5.7 %copy-start.3 = (bf16[8,256,768]{2,1,0:T(8,128)(2,1)S(1)}, bf16[8,256,768]{2,1,0:T(8,128)(2,1)}, u32[]{:S(2)}) copy-start(bf16[8,256,768]{2,1,0:T(8,128)(2,1)} %copy-done.2) | copy-start | bytes 9437188
  298.2 5.7 %copy-start.6 = (bf16[8,256,768]{2,1,0:T(8,128)(2,1)S(1)}, bf16[8,256,768]{2,1,0:T(8,128)(2,1)}, u32[]{:S(2)}) copy-start(bf16[8,256,768]{2,1,0:T(8,128)(2,1)} %get-tuple-element.32) | copy-start | bytes 9437188
  302.8 1.1 copy-start.4
  310.7 145.6 %all-reduce.13.cloned.1.call-start = ((), (), s32[]{:S(2)}) async-start(), calls=%async_computation.5 | async-start | bytes 1179648 | tf_op jit(solution)/shard_map/psum | solution.py:171
  342.0 18.8 %collective-permute-start.2 = (bf16[8,26,384]{2,1,0:T(8,128)(2,1)}, bf16[8,26,384]{2,1,0:T(8,128)(2,1)S(1)}, u32[]{:S(2)}, u32[]{:S(2)}) collective-permute-start(bf16[8,26,384]{2,1,0:T(8,128)(2,1)} %get-tuple-element.38), channel_id=1, source_target_pairs={{8,0},{16,8},{24,16},{9,1},{17,9},{25,17},{10,2},{18,10},{26,18},{... | collective-permute-start | bytes 479240 | tf_op jit(solution)/shard_map/ppermute | solution.py:18
  343.3 17.5 %collective-permute-start.3 = (bf16[8,26,384]{2,1,0:T(8,128)(2,1)}, bf16[8,26,384]{2,1,0:T(8,128)(2,1)S(1)}, u32[]{:S(2)}, u32[]{:S(2)}) collective-permute-start(bf16[8,26,384]{2,1,0:T(8,128)(2,1)} %get-tuple-element.39), channel_id=1, source_target_pairs={{0,8},{8,16},{16,24},{1,9},{9,17},{17,25},{2,10},{10,18},{18,26},{... | collective-permute-start | bytes 479240 | tf_op jit(solution)/shard_map/ppermute | solution.py:15
  360.8 3.1 copy-start.5
  360.8 3.1 copy-start.7
  360.8 3.2 copy-start.13
  360.8 3.2 copy-start.15
  363.9 45.4 %copy-start.10 = (bf16[1,2,8,128]{3,1,2,0:T(2,128)(2,1)S(1)}, bf16[1,2,8,128]{3,1,2,0:T(2,128)(2,1)}, u32[]{:S(2)}) copy-start(bf16[1,2,8,128]{3,1,2,0:T(2,128)(2,1)} %copy-done.9) | copy-start | bytes 12292
  363.9 45.4 %copy-start.16 = (f32[768]{0:T(1024)S(1)}, f32[768]{0:T(1024)}, u32[]{:S(2)}) copy-start(f32[768]{0:T(1024)} %get-tuple-element.28) | copy-start | bytes 9220
Sparse Core Ops, SparseCore 0:
  10.2 29.7 all-gather.1
  251.9 31.9 reduce-scatter.4
  310.9 44.6 reduce-scatter.2
  409.5 46.8 all-reduce.12
where the time goes:
time: 468 us; the launch traced here: 466 us
  blocking collectives  297 us (63%)
  matrix products  44.1 us (9%)
  other arithmetic  41.7 us (9%)
  waiting for transfers between devices  39.1 us (8%)
  local copies, waits for them, and re-layouts  16.4 us (4%)
  between operations  16.2 us (3%)
  starting transfers between devices  11.7 us (2%)
    psum x2, blocking collectives, moments(): lax.psum(jnp.sum(centred * centred * valid, axis=0), ('bins', 'batch', 'f...  83.5 us
    psum x2, blocking collectives, moments(): lax.psum((jnp.sum(values * valid, axis=0), local_count), ('bins', 'batch'...  77.7 us
    psum x2, blocking collectives, norm_back(): lax.psum((jnp.sum(grad_out, axis=0), jnp.sum(grad_out * normed, axis=0)),...  75.6 us
    psum x1, waiting for transfers between devices, local(): summed = lax.psum((local_grads[0], local_grads[1], local_grads[2]), 'bins')  39 us
    unnamed x2, blocking collectives  33.9 us
    all_gather x1, blocking collectives, local(): lax.all_gather(point_weight.astype(bf), ('batch', 'fsdp'), axis=0, tiled=...  15.8 us
    dot_general x2, matrix products, contract_rows(): lax.dot_general(left, right, (((0,), (0,)), ((), ())), preferred_element_...  12.3 us
    psum x1, blocking collectives, local(): summed = lax.psum((local_grads[0], local_grads[1], local_grads[2]), 'bins')  10.6 us
  transfers between devices with their start and end apart: 8, of which 1 were waited for; matrix products, arithmetic and copies ran while one was open for 17% of the time, Pallas kernels for 0%

commit v1 on v0

--- a/solution.py
+++ b/solution.py
@@ -43,7 +43,10 @@
 
 def norm_back(grad_out, normed, scale, gain, valid, count):
     total, cross = lax.psum(
-        (jnp.sum(grad_out, axis=0), jnp.sum(grad_out * normed, axis=0)), ("bins", "batch", "fsdp")
+        lax.psum(
+            (jnp.sum(grad_out, axis=0), jnp.sum(grad_out * normed, axis=0)), ("batch", "fsdp")
+        ),
+        "bins",
     )
     grad_in = scale * gain * (grad_out - valid * (total + normed * cross) / count)
     return (grad_in, total, cross)

time: 468 us -> 421 us (0.90)
  blocking collectives: 297 us -> 255 us
    psum x2, blocking collectives: 75.6 us -> 39.9 us  [norm_back(): lax.psum((jnp.sum(grad_out, axis=0), jnp.sum(grad_out * normed, axis=0)),...]
    unnamed x2 -> x1, blocking collectives: 33.9 us -> 19.1 us
    psum x1 -> x2, blocking collectives: 10.6 us -> 18.9 us  [norm_back(): lax.psum(lax.psum((jnp.sum(grad_out, axis=0), jnp.sum(grad_out * normed,...]
  transfers between devices with their start and end apart: 8 -> 8, of which waited for: 1 -> 1; matrix products, arithmetic and copies ran while one was open for 17% -> 18% of each run, Pallas kernels for 0% -> 0%
where the time goes in v1:
time: 421 us; the launch traced here: 420 us
  blocking collectives  255 us (61%)
  other arithmetic  42.9 us (10%)
  matrix products  42.7 us (10%)
  waiting for transfers between devices  35.4 us (8%)
  local copies, waits for them, and re-layouts  16.4 us (4%)
  between operations  16.2 us (4%)
  starting transfers between devices  11.7 us (3%)
    psum x2, blocking collectives, moments(): lax.psum(jnp.sum(centred * centred * valid, axis=0), ('bins', 'batch', 'f...  83.3 us
    psum x2, blocking collectives, moments(): lax.psum((jnp.sum(values * valid, axis=0), local_count), ('bins', 'batch'...  77.7 us
    psum x2, blocking collectives, norm_back(): lax.psum((jnp.sum(grad_out, axis=0), jnp.sum(grad_out * normed, axis=0)),...  39.9 us
    psum x1, waiting for transfers between devices, local(): summed = lax.psum((local_grads[0], local_grads[1], local_grads[2]), 'bins')  35.4 us
    unnamed x1, blocking collectives  19.1 us
    psum x2, blocking collectives, norm_back(): lax.psum(lax.psum((jnp.sum(grad_out, axis=0), jnp.sum(grad_out * normed,...  18.9 us
    all_gather x1, blocking collectives, local(): lax.all_gather(point_weight.astype(bf), ('batch', 'fsdp'), axis=0, tiled=...  15.9 us
    dot_general x2, matrix products, contract_rows(): lax.dot_general(left, right, (((0,), (0,)), ((), ())), preferred_element_...  12.3 us
  transfers between devices with their start and end apart: 8, of which 1 were waited for; matrix products, arithmetic and copies ran while one was open for 18% of the time, Pallas kernels for 0%

profile of v1, /device:TPU:0, one launch (start us, length us, event | category | flops | bytes accessed | tf_op | source)
XLA Modules:
  0.0 420.2 jit_solution(12789915955542045329)
XLA Ops:
  7.2 1.9 convert_element_type.96
  9.1 0.0 reduce-scatter.5.cloned.1.call-start
  9.2 0.8 fusion.46
  10.0 0.6 convert_reduce_fusion.1
  10.6 0.7 convert_element_type.91
  11.3 0.7 convert_element_type.93
  11.9 0.7 convert_element_type.103
  12.6 1.3 fusion.49
  15.2 0.7 convert_element_type.97
  15.9 0.7 convert_element_type.99
  16.5 0.2 dynamic-update-slice
  16.7 0.2 dynamic-update-slice.1
  16.9 0.2 dynamic-update-slice.4
  17.1 0.2 dynamic-update-slice.2
  17.3 0.2 dynamic-update-slice.3
  17.5 19.1 %all-reduce.12 = (bf16[768]{0:T(1024)(128)(2,1)S(1)}, bf16[768]{0:T(1024)(128)(2,1)S(1)}, bf16[768]{0:T(1024)(128)(2,1)S(1)}, bf16[384]{0:T(512)(128)(2,1)S(1)}, bf16[384]{0:T(512)(128)(2,1)S(1)}) all-reduce(bf16[768]{0:T(1024)(128)(2,1)S(1)} %dynamic-update-slice.4, ...), channel_id=1, replica_groups=mesh['bins'=4,'batch'=4,'fsdp'=2] {'batch','fsdp'}, use_global_device_ids=true, to_apply=%add.4 | all-reduce | flops 3072 | bytes 12288
  36.7 2.6 fusion.13
  39.3 38.0 %all-reduce.6 = (f32[768]{0:T(1024)S(1)}, f32[]{:T(128)}) all-reduce(f32[768]{0:T(1024)S(1)} %fusion.13, f32[]{:T(128)} %convert_reduce_fusion.1), channel_id=1, replica_groups=mesh['bins'=4,'batch'=4,'fsdp'=2] {'bins','batch','fsdp'}, use_global_device_ids=true, to_apply=%region_1.0 | all-reduce | flops 769 | bytes 6152 | tf_op jit(solution)/shard_map/psum | solution.py:33
  77.3 0.6 broadcast_divide_fusion
  78.0 1.1 fusion.3
  79.0 41.6 %psum.117 = f32[768]{0:T(1024)S(1)} all-reduce(f32[768]{0:T(1024)S(1)} %fusion.3), channel_id=1, replica_groups=mesh['bins'=4,'batch'=4,'fsdp'=2] {'bins','batch','fsdp'}, use_global_device_ids=true, to_apply=%region_5.0 | all-reduce | flops 768 | bytes 6144 | tf_op jit(solution)/shard_map/psum | solution.py:38
  120.6 1.2 convert_multiply_fusion.1
  121.9 2.4 fusion.12
  124.3 0.1 fusion.47
  124.4 4.2 %collective-permute-start = (bf16[8,26,768]{2,1,0:T(8,128)(2,1)S(1)}, bf16[8,26,768]{2,1,0:T(8,128)(2,1)S(1)}, u32[]{:S(2)}, u32[]{:S(2)}) collective-permute-start(bf16[8,26,768]{2,1,0:T(8,128)(2,1)S(1)} %get-tuple-element.40), channel_id=1, source_target_pairs={{0,8},{8,16},{16,24},{1,9},{9,17},{17,25},{2,10},{10,18},{18,26},{... | collective-permute-start | bytes 958472 | tf_op jit(solution)/shard_map/ppermute | solution.py:15
  128.6 1.3 collective-permute-start.1
  130.0 2.3 bitcast_multiply_fusion
  132.3 15.9 %all_gather.26 = bf16[384,768]{1,0:T(8,128)(2,1)} all-gather(bf16[48,768]{1,0:T(8,128)(2,1)S(1)} %convert_element_type.102), channel_id=1, replica_groups=mesh['bins'=4,'batch'=4,'fsdp'=2] {'batch','fsdp'}, dimensions={0}, use_global_device_ids=true | all-gather | bytes 663552 | tf_op jit(solution)/shard_map/all_gather | solution.py:80
  148.2 3.6 pad_maximum_fusion.4
  151.8 9.3 %multiply_reduce_fusion.2 = (f32[384]{0:T(512)S(1)}, f32[2048,384]{1,0:T(8,128)}) fusion(f32[2048]{0:T(1024)S(1)} %bitcast.82, bf16[2304,384]{1,0:T(8,128)(2,1)} %all-gather.2.cloned.1.call-done, bf16[2048,768]{1,0:T(8,128)(2,1)} %bitcast.75, bf16[2048,768]{1,0:T(8,128)(2,1)} %bitcast.69, bf16[2048,768]{1,0:T(8,128)(2,1)} %bitcast.73), kind=kOutput, calls=%fused_computation.55 | convolution fusion | flops 3653762560 | bytes 14362112 | tf_op jit(solution)/shard_map/dot_general | solution.py:121
  161.1 39.6 %psum.118 = f32[384]{0:T(512)S(1)} all-reduce(f32[384]{0:T(512)S(1)} %get-tuple-element.51), channel_id=1, replica_groups=mesh['bins'=4,'batch'=4,'fsdp'=2] {'bins','batch','fsdp'}, use_global_device_ids=true, to_apply=%region_7.0 | all-reduce | flops 384 | bytes 3072 | tf_op jit(solution)/shard_map/psum | solution.py:33
  200.8 0.6 broadcast_divide_fusion.1
  201.4 2.3 multiply_reduce_fusion.1
  203.8 41.7 %psum.119 = f32[384]{0:T(512)S(1)} all-reduce(f32[384]{0:T(512)S(1)} %multiply_reduce_fusion.1), channel_id=1, replica_groups=mesh['bins'=4,'batch'=4,'fsdp'=2] {'bins','batch','fsdp'}, use_global_device_ids=true, to_apply=%region_9.0 | all-reduce | flops 384 | bytes 3072 | tf_op jit(solution)/shard_map/psum | solution.py:38
  245.4 0.7 convert_multiply_fusion.2
  246.1 5.5 %fusion.43 = f32[384,768]{1,0:T(8,128)} fusion(bf16[2048,768]{1,0:T(8,128)(2,1)} %bitcast_multiply_fusion, f32[2048,384]{1,0:T(8,128)} %get-tuple-element.52, f32[384]{0:T(512)S(1)} %convert_element_type.100, f32[384]{0:T(512)S(1)} %convert_element_type.98, f32[384]{0:T(512)S(1)} %get-tuple-element.37, f32[384]{0:T(512)S(1)} %broadcast_divide_fusion.1), kind=kOutput, calls=%fused_computation.73 | convolution fusion | flops 1215823872 | bytes 7477248 | tf_op jit(solution)/shard_map/dot_general | solution.py:56
  251.6 0.0 reduce-scatter.3.cloned.1.call-start
  251.7 7.8 %fusion.45 = (f32[384]{0:T(512)S(1)}, f32[384]{0:T(512)S(1)}, f32[2048,384]{1,0:T(8,128)}) fusion(f32[384]{0:T(512)S(1)} %get-tuple-element.37, f32[2048,384]{1,0:T(8,128)} %get-tuple-element.52, f32[384]{0:T(512)S(1)} %broadcast_divide_fusion.1, f32[384]{0:T(512)S(1)} %convert_element_type.100, f32[384]{0:T(512)S(1)} %convert_element_type.98, ...), kind=kOutput, calls=%fused_computation.75 | convolution fusion | flops 1220541696 | bytes 10036224 | tf_op jit(solution)/shard_map/dot_general | solution.py:134
  259.5 14.0 %all-reduce.8 = (f32[384]{0:T(512)S(1)}, f32[384]{0:T(512)S(1)}) all-reduce(f32[384]{0:T(512)S(1)} %get-tuple-element.12, f32[384]{0:T(512)S(1)} %get-tuple-element.11), channel_id=1, replica_groups=mesh['bins'=4,'batch'=4,'fsdp'=2] {'batch','fsdp'}, use_global_device_ids=true, to_apply=%region_14.0 | all-reduce | flops 768 | bytes 6144 | tf_op jit(solution)/shard_map/psum | solution.py:46
  273.5 9.8 %all-reduce.10 = (f32[384]{0:T(512)S(1)}, f32[384]{0:T(512)S(1)}) all-reduce(f32[384]{0:T(512)S(1)} %get-tuple-element.18, f32[384]{0:T(512)S(1)} %get-tuple-element.19), channel_id=1, replica_groups=mesh['bins'=4,'batch'=4,'fsdp'=2] {'bins'}, use_global_device_ids=true, to_apply=%region_15.0 | all-reduce | flops 768 | bytes 6144 | tf_op jit(solution)/shard_map/psum | solution.py:45
  283.3 4.5 %multiply_convert_fusion = bf16[2048,384]{1,0:T(8,128)(2,1)S(1)} fusion(f32[2048,384]{1,0:T(8,128)} %get-tuple-element.53, f32[2048,384]{1,0:T(8,128)} %get-tuple-element.52, f32[]{:T(128)} %get-tuple-element.14, f32[384]{0:T(512)S(1)} %get-tuple-element.23, f32[384]{0:T(512)S(1)} %get-tuple-element.24, f32[384]{0:T(512)S(1)} %get-tuple-element.36, ...), kind=kLoop, calls=%fused_computation.48 | loop fusion | flops 7077888 | bytes 7880196 | tf_op jit(solution)/shard_map/convert_element_type | solution.py:140
  287.9 1.1 copy-done.5
  289.0 6.8 %fusion.36 = f32[2304,384]{1,0:T(8,128)} fusion(bf16[2048,384]{1,0:T(8,128)(2,1)S(1)} %multiply_convert_fusion, bf16[2048,768]{1,0:T(8,128)(2,1)} %bitcast.76, bf16[2048,768]{1,0:T(8,128)(2,1)S(1)} %bitcast.70, bf16[2048,768]{1,0:T(8,128)(2,1)S(1)} %bitcast.74), kind=kOutput, calls=%fused_computation.43 | convolution fusion | flops 3652190208 | bytes 14548992 | tf_op jit(solution)/shard_map/dot_general | solution.py:56
  295.8 0.0 all-reduce.15.cloned.1.call-start
  295.9 0.6 convert_element_type.104
  297.2 3.6 convert_reduce_fusion
  300.8 1.8 fusion.48
  302.6 1.3 collective-permute-start.2
  303.9 4.8 %collective-permute-start.3 = (bf16[8,26,384]{2,1,0:T(8,128)(2,1)}, bf16[8,26,384]{2,1,0:T(8,128)(2,1)S(1)}, u32[]{:S(2)}, u32[]{:S(2)}) collective-permute-start(bf16[8,26,384]{2,1,0:T(8,128)(2,1)} %get-tuple-element.45), channel_id=1, source_target_pairs={{0,8},{8,16},{16,24},{1,9},{9,17},{17,25},{2,10},{10,18},{18,26},{... | collective-permute-start | bytes 479240 | tf_op jit(solution)/shard_map/ppermute | solution.py:15
  308.7 4.9 %fusion.15 = bf16[2048,768]{1,0:T(8,128)(2,1)} fusion(bf16[8,256,768]{2,1,0:T(8,128)(2,1)S(1)} %copy-done, bf16[384,768]{1,0:T(8,128)(2,1)S(1)} %copy-done.9, f32[768]{0:T(1024)S(1)} %copy-done.21, f32[2048,384]{1,0:T(8,128)S(1)} %copy-done.4, f32[384]{0:T(512)} %copy-done.25, f32[384]{0:T(512)} %copy-done.24, f32[384]{0:T(512)} %copy-done.20, ...), kind=kOutput, calls=%fused_computation.20 | convolution fusion | flops 1222115328 | bytes 10036224 | tf_op jit(solution)/shard_map/dot_general | solution.py:125
  313.6 1.2 dynamic_slice.14
  314.8 1.3 dynamic_slice.15
  316.1 3.9 copy.22
  320.0 3.1 pad_maximum_fusion.6
  323.2 8.4 %fusion.44 = (f32[768]{0:T(1024)S(1)}, f32[768]{0:T(1024)S(1)}, f32[2048,768]{1,0:T(8,128)}) fusion(f32[768]{0:T(1024)S(1)} %get-tuple-element.33, f32[768]{0:T(1024)S(1)} %broadcast_divide_fusion, bf16[8,256,768]{2,1,0:T(8,128)(2,1)S(1)} %copy-done, f32[768]{0:T(1024)S(1)} %copy-done.18, f32[768]{0:T(1024)S(1)} %copy-done.16, ...), kind=kOutput, calls=%fused_computation.74 | convolution fusion | flops 3664771584 | bytes 15943680 | tf_op jit(solution)/shard_map/dot_general | solution.py:162
  331.5 25.9 %all-reduce.7 = (f32[768]{0:T(1024)S(1)}, f32[768]{0:T(1024)S(1)}, f32[768]{0:T(1024)S(1)}) all-reduce(f32[768]{0:T(1024)S(1)} %get-tuple-element.10, f32[768]{0:T(1024)S(1)} %get-tuple-element.9, f32[768]{0:T(1024)S(1)} %copy-done.14), channel_id=1, replica_groups=mesh['bins'=4,'batch'=4,'fsdp'=2] {'batch','fsdp'}, use_global_device_ids=true, to_apply=%region_20.0 | all-reduce | flops 2304 | bytes 18432 | tf_op jit(solution)/shard_map/psum | solution.py:46
  357.4 0.1 dynamic-slice.6
  357.5 9.1 %all-reduce.9 = (f32[768]{0:T(1024)S(1)}, f32[768]{0:T(1024)S(1)}, f32[96]{0:T(128)}) all-reduce(f32[768]{0:T(1024)S(1)} %get-tuple-element.15, f32[768]{0:T(1024)S(1)} %get-tuple-element.16, f32[96]{0:T(128)S(1)} %dynamic-slice.6), channel_id=1, replica_groups=mesh['bins'=4,'batch'=4,'fsdp'=2] {'bins'}, use_global_device_ids=true, to_apply=%region_21.0 | all-reduce | flops 1632 | bytes 13056 | tf_op jit(solution)/shard_map/psum | solution.py:45
  366.7 7.1 %fusion.29 = bf16[2048,768]{1,0:T(8,128)(2,1)} fusion(f32[2048,768]{1,0:T(8,128)} %get-tuple-element.54, bf16[8,256,768]{2,1,0:T(8,128)(2,1)S(1)} %copy-done, f32[]{:T(128)} %get-tuple-element.14, f32[768]{0:T(1024)S(1)} %get-tuple-element.20, f32[768]{0:T(1024)S(1)} %get-tuple-element.21, f32[2048]{0:T(1024)S(1)} %bitcast.85, ...), kind=kLoop, calls=%fused_computation.36 | loop fusion | flops 20447232 | bytes 15756292 | tf_op jit(solution)/shard_map/convert_element_type | solution.py:170
  373.7 0.6 dynamic_slice.12
  374.3 0.6 dynamic_slice.13
  374.9 35.4 %all-reduce.15.cloned.1.call-done = (f32[288,384]{1,0:T(8,128)}, f32[48,768]{1,0:T(8,128)}) async-done(((f32[288,384]{1,0:T(8,128)}, f32[48,768]{1,0:T(8,128)}), (f32[288,384]{1,0:T(8,128)}, f32[48,768]{1,0:T(8,128)})) %all-reduce.15.cloned.1.call-update) | async-done | bytes 589840 | tf_op jit(solution)/shard_map/psum | solution.py:174
  410.2 1.8 copy.32
  412.0 1.6 copy.33
  (77 shorter events, 0.3 us)
Async XLA Ops:
  7.2 70.8 %copy-start = (bf16[8,256,768]{2,1,0:T(8,128)(2,1)S(1)}, bf16[8,256,768]{2,1,0:T(8,128)(2,1)}, u32[]{:S(2)}) copy-start(bf16[8,256,768]{2,1,0:T(8,128)(2,1)} %param.12) | copy-start | bytes 9437188
  7.2 144.6 %all-gather.2.cloned.1.call-start = ((), (), s32[]{:S(2)}) async-start(), calls=%async_computation.2 | async-start | bytes 1990656 | tf_op jit(solution)/shard_map/all_gather | solution.py:79
  9.1 357.5 %reduce-scatter.5.cloned.1.call-start = ((), (), s32[]{:S(2)}) async-start(), calls=%async_computation.4 | async-start | bytes 1327104 | tf_op jit(solution)/shard_map/reduce_scatter | solution.py:177
  36.6 85.2 %copy-start.15 = (f32[768]{0:T(1024)}, f32[768]{0:T(1024)S(1)}, u32[]{:S(2)}) copy-start(f32[768]{0:T(1024)S(1)} %convert_element_type.92) | copy-start | bytes 9220
  36.7 85.2 %copy-start.17 = (f32[768]{0:T(1024)}, f32[768]{0:T(1024)S(1)}, u32[]{:S(2)}) copy-start(f32[768]{0:T(1024)S(1)} %convert_element_type.94) | copy-start | bytes 9220
  121.9 8.1 %copy-start.1 = (bf16[8,256,768]{2,1,0:T(8,128)(2,1)S(1)}, bf16[8,256,768]{2,1,0:T(8,128)(2,1)}, u32[]{:S(2)}) copy-start(bf16[8,256,768]{2,1,0:T(8,128)(2,1)} %param.23) | copy-start | bytes 9437188
  124.3 23.9 %copy-start.2 = (bf16[8,256,768]{2,1,0:T(8,128)(2,1)}, bf16[8,256,768]{2,1,0:T(8,128)(2,1)S(1)}, u32[]{:S(2)}) copy-start(bf16[8,256,768]{2,1,0:T(8,128)(2,1)S(1)} %fusion.12) | copy-start | bytes 9437188
  124.4 23.8 %collective-permute-start = (bf16[8,26,768]{2,1,0:T(8,128)(2,1)S(1)}, bf16[8,26,768]{2,1,0:T(8,128)(2,1)S(1)}, u32[]{:S(2)}, u32[]{:S(2)}) collective-permute-start(bf16[8,26,768]{2,1,0:T(8,128)(2,1)S(1)} %get-tuple-element.40), channel_id=1, source_target_pairs={{0,8},{8,16},{16,24},{1,9},{9,17},{17,25},{2,10},{10,18},{18,26},{... | collective-permute-start | bytes 958472 | tf_op jit(solution)/shard_map/ppermute | solution.py:15
  128.6 19.6 %collective-permute-start.1 = (bf16[8,26,768]{2,1,0:T(8,128)(2,1)S(1)}, bf16[8,26,768]{2,1,0:T(8,128)(2,1)S(1)}, u32[]{:S(2)}, u32[]{:S(2)}) collective-permute-start(bf16[8,26,768]{2,1,0:T(8,128)(2,1)S(1)} %get-tuple-element.41), channel_id=1, source_target_pairs={{8,0},{16,8},{24,16},{9,1},{17,9},{25,17},{10,2},{18,10},{26,18},{... | collective-permute-start | bytes 958472 | tf_op jit(solution)/shard_map/ppermute | solution.py:18
  129.9 2.3 copy-start.11
  130.0 2.3 copy-start.10
  132.3 119.4 %copy-start.24 = (f32[384]{0:T(512)}, f32[384]{0:T(512)S(1)}, u32[]{:S(2)}) copy-start(f32[384]{0:T(512)S(1)} %convert_element_type.98) | copy-start | bytes 4612
  132.3 119.4 %copy-start.25 = (f32[384]{0:T(512)}, f32[384]{0:T(512)S(1)}, u32[]{:S(2)}) copy-start(f32[384]{0:T(512)S(1)} %convert_element_type.100) | copy-start | bytes 4612
  201.4 81.9 %copy-start.13 = (f32[384]{0:T(512)}, f32[384]{0:T(512)S(1)}, u32[]{:S(2)}) copy-start(f32[384]{0:T(512)S(1)} %broadcast_divide_fusion.1) | copy-start | bytes 4612
  246.1 37.2 %copy-start.20 = (f32[384]{0:T(512)}, f32[384]{0:T(512)S(1)}, u32[]{:S(2)}) copy-start(f32[384]{0:T(512)S(1)} %get-tuple-element.37) | copy-start | bytes 4612
  251.6 115.0 %reduce-scatter.3.cloned.1.call-start = ((), (), s32[]{:S(2)}) async-start(), calls=%async_computation.3 | async-start | bytes 3981312 | tf_op jit(solution)/shard_map/reduce_scatter | solution.py:176
  283.3 4.6 %copy-start.22 = (f32[384]{0:T(512)}, f32[384]{0:T(512)S(1)}, u32[]{:S(2)}) copy-start(f32[384]{0:T(512)S(1)} %get-tuple-element.24) | copy-start | bytes 4612
  283.3 4.6 %copy-start.23 = (f32[384]{0:T(512)}, f32[384]{0:T(512)S(1)}, u32[]{:S(2)}) copy-start(f32[384]{0:T(512)S(1)} %get-tuple-element.23) | copy-start | bytes 4612
  283.3 5.7 %copy-start.3 = (bf16[8,256,768]{2,1,0:T(8,128)(2,1)S(1)}, bf16[8,256,768]{2,1,0:T(8,128)(2,1)}, u32[]{:S(2)}) copy-start(bf16[8,256,768]{2,1,0:T(8,128)(2,1)} %copy-done.2) | copy-start | bytes 9437188
  283.3 5.7 %copy-start.7 = (bf16[8,256,768]{2,1,0:T(8,128)(2,1)S(1)}, bf16[8,256,768]{2,1,0:T(8,128)(2,1)}, u32[]{:S(2)}) copy-start(bf16[8,256,768]{2,1,0:T(8,128)(2,1)} %get-tuple-element.38) | copy-start | bytes 9437188
  287.9 1.1 copy-start.5
  295.8 114.4 %all-reduce.15.cloned.1.call-start = ((), (), s32[]{:S(2)}) async-start(), calls=%async_computation.5 | async-start | bytes 1179648 | tf_op jit(solution)/shard_map/psum | solution.py:174
  297.1 11.5 %copy-start.4 = (f32[2048,384]{1,0:T(8,128)S(1)}, f32[2048,384]{1,0:T(8,128)}, u32[]{:S(2)}) copy-start(f32[2048,384]{1,0:T(8,128)} %get-tuple-element.52) | copy-start | bytes 9437188
  297.1 11.5 %copy-start.9 = (bf16[384,768]{1,0:T(8,128)(2,1)S(1)}, bf16[384,768]{1,0:T(8,128)(2,1)}, u32[]{:S(2)}) copy-start(bf16[384,768]{1,0:T(8,128)(2,1)} %all_gather.26) | copy-start | bytes 1769476
  297.1 11.5 %copy-start.21 = (f32[768]{0:T(1024)S(1)}, f32[768]{0:T(1024)}, u32[]{:S(2)}) copy-start(f32[768]{0:T(1024)} %convert_element_type.104) | copy-start | bytes 9220
  302.6 17.4 %collective-permute-start.2 = (bf16[8,26,384]{2,1,0:T(8,128)(2,1)}, bf16[8,26,384]{2,1,0:T(8,128)(2,1)S(1)}, u32[]{:S(2)}, u32[]{:S(2)}) collective-permute-start(bf16[8,26,384]{2,1,0:T(8,128)(2,1)} %get-tuple-element.44), channel_id=1, source_target_pairs={{8,0},{16,8},{24,16},{9,1},{17,9},{25,17},{10,2},{18,10},{26,18},{... | collective-permute-start | bytes 479240 | tf_op jit(solution)/shard_map/ppermute | solution.py:18
  303.9 16.1 %collective-permute-start.3 = (bf16[8,26,384]{2,1,0:T(8,128)(2,1)}, bf16[8,26,384]{2,1,0:T(8,128)(2,1)S(1)}, u32[]{:S(2)}, u32[]{:S(2)}) collective-permute-start(bf16[8,26,384]{2,1,0:T(8,128)(2,1)} %get-tuple-element.45), channel_id=1, source_target_pairs={{0,8},{8,16},{16,24},{1,9},{9,17},{17,25},{2,10},{10,18},{18,26},{... | collective-permute-start | bytes 479240 | tf_op jit(solution)/shard_map/ppermute | solution.py:15
  319.9 3.2 copy-start.6
  319.9 3.2 copy-start.8
  320.0 3.2 copy-start.16
  320.0 3.2 copy-start.18
  323.1 8.4 %copy-start.14 = (f32[768]{0:T(1024)S(1)}, f32[768]{0:T(1024)}, u32[]{:S(2)}) copy-start(f32[768]{0:T(1024)} %convert_reduce_fusion) | copy-start | bytes 9220
  323.2 43.5 %copy-start.12 = (bf16[1,2,8,128]{3,1,2,0:T(2,128)(2,1)S(1)}, bf16[1,2,8,128]{3,1,2,0:T(2,128)(2,1)}, u32[]{:S(2)}) copy-start(bf16[1,2,8,128]{3,1,2,0:T(2,128)(2,1)} %copy-done.11) | copy-start | bytes 12292
  323.2 43.5 %copy-start.19 = (f32[768]{0:T(1024)S(1)}, f32[768]{0:T(1024)}, u32[]{:S(2)}) copy-start(f32[768]{0:T(1024)} %get-tuple-element.32) | copy-start | bytes 9220
Sparse Core Ops, SparseCore 0:
  10.2 29.7 all-gather.1
  251.7 32.1 reduce-scatter.4
  295.9 40.6 reduce-scatter.2
  366.8 43.4 all-reduce.14
